TPU v7x, 32 devices: a whole 2x2x4 slice. The times are simulated.
32 devices in a mesh: dom: 8 (over z, core), cls: 4 (over y, x).
Axes of the slice: x: 2, y: 2, z: 4, core: 2. Of those that a mesh axis runs over, the one named last changes fastest.
Arguments:
- particles: bfloat16 [768, 2048], P('dom', 'cls'), may hold values from -12 to 12
- references: float32 [32, 36, 2048], P('cls', None, 'dom'), may hold values from -0.4 to 0.4
- noise_weight: float32 [1024], replicated, may hold values from 0.5 to 2
Outputs:
- class_sums: float32 [32, 36, 2048], P('cls', None, 'dom')
- class_weight: float32 [32, 36], P('cls')
All inputs are finite; a program needn't handle non-finite values.
Results may differ from a plain program's by a relative error of at most 0.0033.
Values may be sent and summed in bfloat16 or wider, within the bound.
No kernel may reach another device: no remote copies, remote signals or barrier semaphores. Data moves between devices by JAX's collectives and lax.ppermute only.
A program may use at most 64 MiB of HBM per device.

v0:
```python
import math
import jax
import jax.numpy as jnp
from jax import lax
from jax.sharding import PartitionSpec as P

WIN = 32
BOX = 64
SHIFT_SIDE = 9


def phase_tables():
    freq = jnp.arange(WIN * WIN)
    freq_y = (freq // WIN - WIN // 2).astype(jnp.float32)
    freq_x = (freq % WIN - WIN // 2).astype(jnp.float32)
    offset = jnp.arange(SHIFT_SIDE * SHIFT_SIDE)
    shift_y = (offset // SHIFT_SIDE - SHIFT_SIDE // 2).astype(jnp.float32)
    shift_x = (offset % SHIFT_SIDE - SHIFT_SIDE // 2).astype(jnp.float32)
    theta = (
        2.0
        * math.pi
        / BOX
        * (shift_x[:, None] * freq_x[None, :] + shift_y[:, None] * freq_y[None, :])
    )
    return (jnp.cos(theta), jnp.sin(theta))


def shifted_block(real_part, imag_part, cosine, sine):
    moved_real = real_part[None] * cosine[:, None] + imag_part[None] * sine[:, None]
    moved_imag = imag_part[None] * cosine[:, None] - real_part[None] * sine[:, None]
    return jnp.concatenate([moved_real, moved_imag], axis=2).astype(jnp.bfloat16)


def on_device(particles, references, noise_weight):
    columns = lax.all_gather(particles, "cls", axis=1, tiled=True)
    quarter = WIN * WIN
    real_part = columns[:, :quarter].astype(jnp.float32)
    imag_part = columns[:, quarter:].astype(jnp.float32)
    weight_full = jnp.concatenate([noise_weight, noise_weight])
    gathered = lax.all_gather(references, "dom", axis=2, tiled=True)
    weighted = (gathered * weight_full).astype(jnp.bfloat16)
    half_norm = 0.5 * jnp.sum(gathered * gathered * weight_full, axis=2)
    classes_here = weighted.shape[0]
    rotations = weighted.shape[1]
    hypotheses = classes_here * rotations
    ref_matrix = weighted.reshape(hypotheses, -1)
    half_flat = half_norm.reshape(hypotheses)
    cosine, sine = phase_tables()
    block_shifts = 3
    blocks = cosine.shape[0] // block_shifts
    rows_here = particles.shape[0]

    def block_scores(index, ref_rows, half_rows):
        cos_block = lax.dynamic_slice_in_dim(cosine, index * block_shifts, block_shifts)
        sin_block = lax.dynamic_slice_in_dim(sine, index * block_shifts, block_shifts)
        moved = shifted_block(real_part, imag_part, cos_block, sin_block)
        flat = moved.reshape(block_shifts * rows_here, -1)
        scores = (
            lax.dot_general(
                flat, ref_rows, (((1,), (1,)), ((), ())), preferred_element_type=jnp.float32
            )
            - half_rows
        )
        return (flat, scores.reshape(block_shifts, rows_here, ref_rows.shape[0]))

    def first_pass(index, carry):
        top, total = carry
        _, scores = block_scores(index, ref_matrix, half_flat)
        new_top = jnp.maximum(top, jnp.max(scores, axis=(0, 2)))
        total = total * jnp.exp(top - new_top) + jnp.sum(
            jnp.exp(scores - new_top[None, :, None]), axis=(0, 2)
        )
        return (new_top, total)

    start = (jnp.full((rows_here,), -jnp.inf, jnp.float32), jnp.zeros((rows_here,), jnp.float32))
    top, total = lax.fori_loop(0, blocks, first_pass, start)
    global_top = lax.pmax(top, "cls")
    total = lax.psum(total * jnp.exp(top - global_top), "cls")
    top = global_top
    count = ref_matrix.shape[0]

    def second_pass(index, carry):
        sums, weights_total = carry
        flat, scores = block_scores(index, ref_matrix, half_flat)
        probs = jnp.exp(scores - top[None, :, None]) / total[None, :, None]
        probs_low = probs.astype(jnp.bfloat16).reshape(block_shifts * rows_here, count)
        sums = sums + lax.dot_general(
            probs_low, flat, (((0,), (0,)), ((), ())), preferred_element_type=jnp.float32
        )
        weights_total = weights_total + jnp.sum(probs, axis=(0, 1))
        return (sums, weights_total)

    start_two = (
        jnp.zeros((count, ref_matrix.shape[1]), jnp.float32),
        jnp.zeros((count,), jnp.float32),
    )
    sums, weights_total = lax.fori_loop(0, blocks, second_pass, start_two)
    class_sums = lax.psum_scatter(
        sums.reshape(classes_here, rotations, -1), "dom", scatter_dimension=2, tiled=True
    )
    class_weight = lax.psum(weights_total, "dom").reshape(classes_here, rotations)
    return (class_sums, class_weight)


def solution(mesh):
    placed = (P("dom", "cls"), P("cls", None, "dom"), P())
    return jax.shard_map(
        on_device,
        mesh=mesh,
        in_specs=placed,
        out_specs=(P("cls", None, "dom"), P("cls", None)),
        check_vma=False,
    )
```

profile of v0, /device:TPU:0, one launch (start us, length us, event | category | flops | bytes accessed | tf_op | source)
XLA Modules:
  0.0 489.8 jit_solution(18415613660315926192)
XLA Ops:
  8.0 11.3 %all_gather.6 = bf16[96,2048]{1,0:T(8,128)(2,1)S(1)} all-gather(bf16[96,512]{1,0:T(8,128)(2,1)} %param.7), channel_id=1, replica_groups=mesh['dom'=8,'cls'=4] {'cls'}, dimensions={1}, use_global_device_ids=true | all-gather | bytes 491520 | tf_op jit(solution)/shard_map/all_gather | solution.py:35
  20.7 2.2 fusion.19
  23.9 20.1 %all-gather.2.cloned.1.call-done = f32[8,36,2048]{2,0,1:T(8,128)} async-done(((f32[8,36,256]{2,0,1:T(8,128)}), f32[8,36,2048]{2,0,1:T(8,128)}) %all-gather.2.cloned.1.call-update) | async-done | bytes 2359312 | tf_op jit(solution)/shard_map/all_gather | solution.py:40
  50.5 2.2 reshape.155
  52.8 100.0 %while.34 = (s32[]{:T(128)}, f32[96]{0:T(128)S(1)}, f32[96]{0:T(128)S(1)}, f32[96,1024]{1,0:T(8,128)}, f32[81,1024]{1,0:T(8,128)}, /*index=5*/f32[96,1024]{1,0:T...) while((s32[]{:T(128)}, f32[96]{0:T(128)S(1)}, ...), condition=%wide.wide.region_6.7_spmd.clone, body=%wide.wide.region_1.6_spmd.clone.sunk | while | flops 344789472 | bytes 9801470 | solution.py:76
  152.8 9.8 %pmax.7 = f32[96]{0:T(128)S(1)} all-reduce(f32[96]{0:T(128)S(1)} %get-tuple-element.342), channel_id=1, replica_groups=mesh['dom'=8,'cls'=4] {'cls'}, use_global_device_ids=true, to_apply=%region_7.8 | all-reduce | flops 96 | bytes 768 | tf_op jit(solution)/shard_map/pmax | solution.py:77
  162.6 8.0 %psum.14 = f32[96]{0:T(128)S(1)} all-reduce(f32[96]{0:T(128)S(1)} %exponential_multiply_fusion), channel_id=1, replica_groups=mesh['dom'=8,'cls'=4] {'cls'}, use_global_device_ids=true, to_apply=%region_8.9 | all-reduce | flops 96 | bytes 768 | tf_op jit(solution)/shard_map/psum | solution.py:78
  170.6 272.8 %while.35 = (s32[]{:T(128)}, f32[288,2048]{1,0:T(8,128)S(1)}, f32[288]{0:T(512)S(1)}, f32[96,1024]{1,0:T(8,128)}, f32[81,1024]{1,0:T(8,128)}, /*index=5*/f32[96,...) while((s32[]{:T(128)}, f32[288,2048]{1,0:T(8,128)S(1)}, ...), condition=%wide.wide.region_11.12_spmd.clone, body=%wide.wide.region_9.11_spmd.clone.sunk | while | flops 688315712 | bytes 16369070 | solution.py:97
  214.2 2.2 fusion.59
  224.3 2.2 fusion.59
  234.4 2.2 fusion.59
  244.5 2.2 fusion.59
  274.8 2.2 fusion.59
  285.0 2.2 fusion.59
  295.1 2.2 fusion.59
  305.2 2.2 fusion.59
  315.3 2.2 fusion.59
  335.5 2.2 fusion.59
  345.6 2.2 fusion.59
  355.7 2.2 fusion.59
  365.8 2.2 fusion.59
  375.9 2.2 fusion.59
  445.2 14.5 %psum.15 = f32[8,36]{1,0:T(8,128)} all-reduce(f32[8,36]{1,0:T(8,128)S(1)} %reshape.157), channel_id=1, replica_groups=mesh['dom'=8,'cls'=4] {'dom'}, use_global_device_ids=true, to_apply=%region_13.14 | all-reduce | flops 288 | bytes 2304 | tf_op jit(solution)/shard_map/psum | solution.py:101
  459.7 21.4 %reduce-scatter.2.cloned.1.call-done = f32[8,36,256]{2,1,0:T(8,128)} async-done(((f32[8,36,2048]{2,1,0:T(8,128)}), f32[8,36,256]{2,1,0:T(8,128)}) %reduce-scatter.2.cloned.1.call-update) | async-done | bytes 294928 | tf_op jit(solution)/shard_map/reduce_scatter | solution.py:98
  (851 shorter events, 351.9 us)
Async XLA Ops:
  7.2 36.8 %all-gather.2.cloned.1.call-start = ((), (), s32[]{:S(2)}) async-start(), calls=%async_computation.1 | async-start | bytes 2654208 | tf_op jit(solution)/shard_map/all_gather | solution.py:40
  7.9 473.2 %reduce-scatter.2.cloned.1.call-start = ((), (), s32[]{:S(2)}) async-start(), calls=%async_computation.2 | async-start | bytes 2949120 | tf_op jit(solution)/shard_map/reduce_scatter | solution.py:98
  47.5 3.1 copy-start.3
  171.4 2.4 copy-start.5
  181.5 2.4 copy-start.5
  191.6 2.4 copy-start.5
  201.7 2.4 copy-start.5
  211.8 2.4 copy-start.5
  221.9 2.4 copy-start.5
  232.0 2.4 copy-start.5
  242.1 2.4 copy-start.5
  252.2 2.4 copy-start.5
  262.3 2.4 copy-start.5
  272.4 2.4 copy-start.5
  282.5 2.4 copy-start.5
  292.6 2.4 copy-start.5
  302.7 2.4 copy-start.5
  312.8 2.4 copy-start.5
  322.9 2.4 copy-start.5
  333.0 2.4 copy-start.5
  343.2 2.4 copy-start.5
  363.4 2.4 copy-start.5
  373.5 2.4 copy-start.5
  434.1 2.4 copy-start.5
  (89 other events, 214.5 us)
Sparse Core Ops, SparseCore 0:
  9.6 34.3 all-gather.1
  445.2 35.8 reduce-scatter.1
where the time goes:
time: 495 us; the launch traced here: 490 us
  local copies, waits for them, and re-layouts  144 us (29%)
  matrix products  135 us (27%)
  other arithmetic  107 us (22%)
  blocking collectives  43.6 us (9%)
  waiting for transfers between devices  42.2 us (9%)
  between operations  14.1 us (3%)
    dot_general x54, matrix products, block_scores(): lax.dot_general(flat, ref_rows, (((1,), (1,)), ((), ())), preferred_eleme...  80.1 us
    another operation x54, other arithmetic  76.2 us
    dot_general x27, matrix products, second_pass(): lax.dot_general(probs_low, flat, (((0,), (0,)), ((), ())), preferred_elem...  55.1 us
    reshape x27, local copies, waits for them, and re-layouts, block_scores(): return (flat, scores.reshape(block_shifts, rows_here, ref_rows.shape[0]))  53.6 us
    dynamic_slice x54, local copies, waits for them, and re-layouts, block_scores(): lax.dynamic_slice_in_dim(sine, index * block_shifts, block_shifts)  52.9 us
    reduce_scatter x1, waiting for transfers between devices, on_device(): lax.psum_scatter(sums.reshape(classes_here, rotations, -1), 'dom', scatte...  21.4 us
    all_gather x1, waiting for transfers between devices, on_device(): gathered = lax.all_gather(references, 'dom', axis=2, tiled=True)  20.1 us
    add x27, other arithmetic, second_pass(): weights_total = weights_total + jnp.sum(probs, axis=(0, 1))  18.6 us
  transfers between devices with their start and end apart: 2, of which 2 were waited for; matrix products, arithmetic and copies ran while one was open for 1% of the time, Pallas kernels for 0%

commit v1 on v0

--- a/solution.py
+++ b/solution.py
@@ -7,6 +7,12 @@
 WIN = 32
 BOX = 64
 SHIFT_SIDE = 9
+
+
+def joined_along(pieces, dim):
+    pieces = jnp.moveaxis(pieces, 0, dim)
+    shape = pieces.shape
+    return pieces.reshape(*shape[:dim], shape[dim] * shape[dim + 1], *shape[dim + 2 :])
 
 
 def phase_tables():
@@ -37,7 +43,19 @@
     real_part = columns[:, :quarter].astype(jnp.float32)
     imag_part = columns[:, quarter:].astype(jnp.float32)
     weight_full = jnp.concatenate([noise_weight, noise_weight])
-    gathered = lax.all_gather(references, "dom", axis=2, tiled=True)
+    length = lax.axis_size("dom")
+    pairs = [(i, (i + 1) % length) for i in range(length)]
+    back = [(b, a) for a, b in pairs]
+    lower, upper = ([], [])
+    for lap in range(length - 1):
+        if lap % 2 == 0:
+            lower.append(lax.ppermute(lower[-1] if lower else references, "dom", pairs))
+        else:
+            upper.append(lax.ppermute(upper[-1] if upper else references, "dom", back))
+    blocks_2 = jnp.stack([*lower[::-1], references, *upper])
+    shift = lax.axis_index("dom") - len(lower)
+    blocks_2 = blocks_2[(jnp.arange(length) - shift) % length]
+    gathered = joined_along(blocks_2, 2)
     weighted = (gathered * weight_full).astype(jnp.bfloat16)
     half_norm = 0.5 * jnp.sum(gathered * gathered * weight_full, axis=2)
     classes_here = weighted.shape[0]

time: 495 us -> 571 us (1.15)
  matrix products: 135 us -> 204 us
  waiting for transfers between devices: 42.2 us -> 30.1 us
  starting transfers between devices: 0.08 us -> 10.6 us
    dot_general x54, matrix products: 80.1 us -> 149 us  [block_scores(): lax.dot_general(flat, ref_rows, (((1,), (1,)), ((), ())), preferred_eleme...]
    all_gather x1 -> x0, waiting for transfers between devices: 20.1 us -> none  [on_device(): gathered = lax.all_gather(references, 'dom', axis=2, tiled=True)]
    ppermute x0 -> x7, starting transfers between devices: none -> 10.5 us  [the longest x3 10 us: on_device(): upper.append(lax.ppermute(upper[-1] if upper else references, 'dom', back))]
    ppermute x0 -> x7, waiting for transfers between devices: none -> 10 us  [the longest x4 10 us: on_device(): lower.append(lax.ppermute(lower[-1] if lower else references, 'dom', pairs))]
  transfers between devices with their start and end apart: 2 -> 8, of which waited for: 2 -> 4; matrix products, arithmetic and copies ran while one was open for 1% -> 2% of each run, Pallas kernels for 0% -> 0%
where the time goes in v1:
time: 571 us; the launch traced here: 563 us
  matrix products  204 us (36%)
  local copies, waits for them, and re-layouts  148 us (26%)
  other arithmetic  110 us (19%)
  blocking collectives  42.6 us (7%)
  waiting for transfers between devices  30.1 us (5%)
  between operations  14.1 us (2%)
  starting transfers between devices  10.6 us (2%)
    dot_general x54, matrix products, block_scores(): lax.dot_general(flat, ref_rows, (((1,), (1,)), ((), ())), preferred_eleme...  149 us
    another operation x54, other arithmetic  76.2 us
    dot_general x27, matrix products, second_pass(): lax.dot_general(probs_low, flat, (((0,), (0,)), ((), ())), preferred_elem...  54.9 us
    reshape x27, local copies, waits for them, and re-layouts, block_scores(): return (flat, scores.reshape(block_shifts, rows_here, ref_rows.shape[0]))  54 us
    dynamic_slice x54, local copies, waits for them, and re-layouts, block_scores(): lax.dynamic_slice_in_dim(sine, index * block_shifts, block_shifts)  47.8 us
    reduce_scatter x1, waiting for transfers between devices, on_device(): lax.psum_scatter(sums.reshape(classes_here, rotations, -1), 'dom', scatte...  20.1 us
    add x27, other arithmetic, second_pass(): weights_total = weights_total + jnp.sum(probs, axis=(0, 1))  18.5 us
    sub x54, local copies, waits for them, and re-layouts, second_pass(): probs = jnp.exp(scores - top[None, :, None]) / total[None, :, None]  18 us
  transfers between devices with their start and end apart: 8, of which 4 were waited for; matrix products, arithmetic and copies ran while one was open for 2% of the time, Pallas kernels for 0%

profile of v1, /device:TPU:0, one launch (start us, length us, event | category | flops | bytes accessed | tf_op | source)
XLA Modules:
  0.0 562.5 jit_solution(711071138619459089)
XLA Ops:
  7.7 4.1 collective-permute-start.4
  18.7 6.1 %collective-permute-done.1 = f32[8,36,256]{2,0,1:T(8,128)S(1)} collective-permute-done((f32[8,36,256]{2,0,1:T(8,128)S(1)}, f32[8,36,256]{2,0,1:T(8,128)S(1)}, u32[]{:S(2)}, u32[]{:S(2)}) %collective-permute-start.1) | collective-permute-done | bytes 294944 | tf_op jit(solution)/shard_map/ppermute | solution.py:52
  28.5 3.5 collective-permute-start.5
  32.9 10.8 %all_gather.3 = bf16[96,2048]{1,0:T(8,128)(2,1)S(1)} all-gather(bf16[96,512]{1,0:T(8,128)(2,1)} %param.7), channel_id=1, replica_groups=mesh['dom'=8,'cls'=4] {'cls'}, dimensions={1}, use_global_device_ids=true | all-gather | bytes 491520 | tf_op jit(solution)/shard_map/all_gather | solution.py:41
  52.9 3.9 gather_fusion
  65.0 131.2 %while.34 = (s32[]{:T(128)}, f32[96]{0:T(128)S(1)}, f32[96]{0:T(128)S(1)}, f32[96,1024]{1,0:T(8,128)}, f32[81,1024]{1,0:T(8,128)}, /*index=5*/f32[96,1024]{1,0:T...) while((s32[]{:T(128)}, f32[96]{0:T(128)S(1)}, ...), condition=%wide.wide.region_6.7_spmd.clone, body=%wide.wide.region_1.6_spmd.clone.sunk | while | flops 344789472 | bytes 5082850 | solution.py:94
  196.2 8.9 %pmax.7 = f32[96]{0:T(128)S(1)} all-reduce(f32[96]{0:T(128)S(1)} %get-tuple-element.342), channel_id=1, replica_groups=mesh['dom'=8,'cls'=4] {'cls'}, use_global_device_ids=true, to_apply=%region_7.8 | all-reduce | flops 96 | bytes 768 | tf_op jit(solution)/shard_map/pmax | solution.py:95
  205.1 8.3 %psum.14 = f32[96]{0:T(128)S(1)} all-reduce(f32[96]{0:T(128)S(1)} %exponential_multiply_fusion), channel_id=1, replica_groups=mesh['dom'=8,'cls'=4] {'cls'}, use_global_device_ids=true, to_apply=%region_8.9 | all-reduce | flops 96 | bytes 768 | tf_op jit(solution)/shard_map/psum | solution.py:96
  213.4 304.1 %while.35 = (s32[]{:T(128)}, f32[288,2048]{1,0:T(8,128)S(1)}, f32[288]{0:T(512)S(1)}, f32[96,1024]{1,0:T(8,128)}, f32[81,1024]{1,0:T(8,128)}, /*index=5*/f32[96,...) while((s32[]{:T(128)}, f32[288,2048]{1,0:T(8,128)S(1)}, ...), condition=%wide.wide.region_11.12_spmd.clone, body=%wide.wide.region_9.11_spmd.clone.sunk | while | flops 688315712 | bytes 11641178 | solution.py:115
  216.5 3.4 fusion.61
  239.0 3.4 fusion.61
  261.5 3.4 fusion.61
  284.1 3.4 fusion.61
  306.6 3.4 fusion.61
  329.1 3.4 fusion.61
  351.6 3.4 fusion.61
  374.2 3.4 fusion.61
  396.7 3.4 fusion.61
  419.2 3.4 fusion.61
  441.7 3.4 fusion.61
  464.3 3.4 fusion.61
  486.8 3.4 fusion.61
  519.2 14.6 %psum.15 = f32[8,36]{1,0:T(8,128)} all-reduce(f32[8,36]{1,0:T(8,128)S(1)} %reshape.211), channel_id=1, replica_groups=mesh['dom'=8,'cls'=4] {'dom'}, use_global_device_ids=true, to_apply=%region_13.14 | all-reduce | flops 288 | bytes 2304 | tf_op jit(solution)/shard_map/psum | solution.py:119
  533.8 20.1 %reduce-scatter.2.cloned.1.call-done = f32[8,36,256]{2,1,0:T(8,128)} async-done(((f32[8,36,2048]{2,1,0:T(8,128)}), f32[8,36,256]{2,1,0:T(8,128)}) %reduce-scatter.2.cloned.1.call-update) | async-done | bytes 294928 | tf_op jit(solution)/shard_map/reduce_scatter | solution.py:116
  (662 shorter events, 420.4 us)
Async XLA Ops:
  7.2 546.8 %reduce-scatter.2.cloned.1.call-start = ((), (), s32[]{:S(2)}) async-start(), calls=%async_computation.1 | async-start | bytes 2949120 | tf_op jit(solution)/shard_map/reduce_scatter | solution.py:116
  7.2 9.7 %collective-permute-start = (f32[8,36,256]{2,0,1:T(8,128)}, f32[8,36,256]{2,0,1:T(8,128)S(1)}, u32[]{:S(2)}, u32[]{:S(2)}) collective-permute-start(f32[8,36,256]{2,0,1:T(8,128)} %param.8), channel_id=1, source_target_pairs={{0,4},{4,8},{8,12},{12,16},{16,20},{20,24},{24,28},{28,0},{1,5},{5... | collective-permute-start | bytes 884744 | tf_op jit(solution)/shard_map/ppermute | solution.py:52
  7.7 20.7 %collective-permute-start.4 = (f32[8,36,256]{2,0,1:T(8,128)}, f32[8,36,256]{2,0,1:T(8,128)S(1)}, u32[]{:S(2)}, u32[]{:S(2)}) collective-permute-start(f32[8,36,256]{2,0,1:T(8,128)} %param.8), channel_id=1, source_target_pairs={{4,0},{8,4},{12,8},{16,12},{20,16},{24,20},{28,24},{0,28},{5,1},{9... | collective-permute-start | bytes 884744 | tf_op jit(solution)/shard_map/ppermute | solution.py:54
  16.9 7.9 %collective-permute-start.1 = (f32[8,36,256]{2,0,1:T(8,128)S(1)}, f32[8,36,256]{2,0,1:T(8,128)S(1)}, u32[]{:S(2)}, u32[]{:S(2)}) collective-permute-start(f32[8,36,256]{2,0,1:T(8,128)S(1)} %collective-permute-done), channel_id=1, source_target_pairs={{0,4},{4,8},{8,12},{12,16},{16,20},{20,24},{24,28},{28,0},{1,5},{5... | collective-permute-start | bytes 884744 | tf_op jit(solution)/shard_map/ppermute | solution.py:52
  24.8 8.1 %collective-permute-start.2 = (f32[8,36,256]{2,0,1:T(8,128)S(1)}, f32[8,36,256]{2,0,1:T(8,128)S(1)}, u32[]{:S(2)}, u32[]{:S(2)}) collective-permute-start(f32[8,36,256]{2,0,1:T(8,128)S(1)} %collective-permute-done.1), channel_id=1, source_target_pairs={{0,4},{4,8},{8,12},{12,16},{16,20},{20,24},{24,28},{28,0},{1,5},{5... | collective-permute-start | bytes 884744 | tf_op jit(solution)/shard_map/ppermute | solution.py:52
  25.4 24.6 %copy-start = (f32[8,36,256]{2,0,1:T(8,128)S(1)}, f32[8,36,256]{2,0,1:T(8,128)}, u32[]{:S(2)}) copy-start(f32[8,36,256]{2,0,1:T(8,128)} %param.8) | copy-start | bytes 884740
  28.5 16.2 %collective-permute-start.5 = (f32[8,36,256]{2,0,1:T(8,128)S(1)}, f32[8,36,256]{2,0,1:T(8,128)S(1)}, u32[]{:S(2)}, u32[]{:S(2)}) collective-permute-start(f32[8,36,256]{2,0,1:T(8,128)S(1)} %collective-permute-done.4), channel_id=1, source_target_pairs={{4,0},{8,4},{12,8},{16,12},{20,16},{24,20},{28,24},{0,28},{5,1},{9... | collective-permute-start | bytes 884744 | tf_op jit(solution)/shard_map/ppermute | solution.py:54
  32.9 14.2 %collective-permute-start.3 = (f32[8,36,256]{2,0,1:T(8,128)S(1)}, f32[8,36,256]{2,0,1:T(8,128)S(1)}, u32[]{:S(2)}, u32[]{:S(2)}) collective-permute-start(f32[8,36,256]{2,0,1:T(8,128)S(1)} %collective-permute-done.2), channel_id=1, source_target_pairs={{0,4},{4,8},{8,12},{12,16},{16,20},{20,24},{24,28},{28,0},{1,5},{5... | collective-permute-start | bytes 884744 | tf_op jit(solution)/shard_map/ppermute | solution.py:52
  44.7 7.5 %collective-permute-start.6 = (f32[8,36,256]{2,0,1:T(8,128)S(1)}, f32[8,36,256]{2,0,1:T(8,128)S(1)}, u32[]{:S(2)}, u32[]{:S(2)}) collective-permute-start(f32[8,36,256]{2,0,1:T(8,128)S(1)} %collective-permute-done.5), channel_id=1, source_target_pairs={{4,0},{8,4},{12,8},{16,12},{20,16},{24,20},{28,24},{0,28},{5,1},{9... | collective-permute-start | bytes 884744 | tf_op jit(solution)/shard_map/ppermute | solution.py:54
  52.9 3.9 copy-start.3
  58.9 3.8 copy-start.1
  62.7 1.0 copy-start.2
Sparse Core Ops, SparseCore 0:
  519.3 34.5 reduce-scatter.1
